TPU v7x, 32 devices: a whole 2x2x4 slice. The times are simulated.
32 devices in a mesh: ctx: 8 (over z, x), fsdp: 4 (over y, core).
Axes of the slice: x: 2, y: 2, z: 4, core: 2. Of those that a mesh axis runs over, the one named last changes fastest.
Arguments:
- hidden: bfloat16 [8, 1024, 1024], P('fsdp', 'ctx'), may hold values from -6 to 6
- segment_ids: int32 [8, 1024], P('fsdp', 'ctx'), may hold values from 0 to 3, never falling along the last dimension, each value on 1 to 512 neighbouring positions
- cotangent: bfloat16 [8, 1024, 1024], P('fsdp', 'ctx'), may hold values from -6 to 6
- w_qkv: bfloat16 [1024, 3072], P('fsdp'), may hold values from -0.1875 to 0.1875
- w_attn_out: bfloat16 [1024, 1024], P('fsdp'), may hold values from -3 to 3
- w_in: bfloat16 [1024, 5248], P('fsdp'), may hold values from -0.1875 to 0.1875
- w_mlp_out: bfloat16 [2624, 1024], P('fsdp'), may hold values from -0.15625 to 0.15625
- gain_attn: bfloat16 [1024], P('fsdp'), may hold values from 0.099609375 to 1.8984375
- gain_mlp: bfloat16 [1024], P('fsdp'), may hold values from 0.099609375 to 1.8984375
Outputs:
- output: bfloat16 [8, 1024, 1024], P('fsdp', 'ctx')
- input_grad: float32 [8, 1024, 1024], P('fsdp', 'ctx')
- grad_w_qkv: float32 [1024, 3072], P('fsdp')
- grad_w_attn_out: float32 [1024, 1024], P('fsdp')
- grad_w_in: float32 [1024, 5248], P('fsdp')
- grad_w_mlp_out: float32 [2624, 1024], P('fsdp')
- grad_gain_attn: float32 [1024], P('fsdp')
- grad_gain_mlp: float32 [1024], P('fsdp')
Inputs may be any that keep to these rules, and one draw needn't show every extreme that they name: `segment_ids`: along each sequence the document numbers never fall; every document spans at most half of 1024 positions, and one in each sequence spans exactly that many.
All inputs are finite; a program needn't handle non-finite values.
Results may differ from a plain program's by a relative error of at most 0.024.
Values may be sent and summed in bfloat16 or wider, within the bound.
No kernel may reach another device: no remote copies, remote signals or barrier semaphores. Data moves between devices by JAX's collectives and lax.ppermute only.
A program may use at most 192 MiB of HBM per device.

v0:
```python
import jax
import jax.numpy as jnp
from jax import lax
from jax.sharding import PartitionSpec as P

HEADS = 16
MICRO = 2
rope_base = 160000.0
norm_eps = 1e-05
masked_score = -1e30


def shortened(value):
    return jax.tree.map(lambda a: a.astype(jnp.bfloat16) if a.dtype == jnp.float32 else a, value)


def norm_scale(values, gain):
    center = values - jnp.mean(values, axis=-1, keepdims=True)
    spread = jnp.mean(center * center, axis=-1, keepdims=True)
    return center * lax.rsqrt(spread + norm_eps) * gain


def rope_tables(positions, head_size):
    half = head_size // 2
    inverse = rope_base ** (-(jnp.arange(half, dtype=jnp.float32) * 2.0 / head_size))
    angles = positions.astype(jnp.float32)[:, None] * inverse[None, :]
    return (jnp.cos(angles), jnp.sin(angles))


def rotate_heads(values, cosine, sine, heads):
    shape = values.shape
    split = values.reshape(shape[:-1] + (heads, shape[-1] // heads))
    half = split.shape[-1] // 2
    first = split[..., :half]
    second = split[..., half:]
    cos_heads = cosine[:, None, :]
    sin_heads = sine[:, None, :]
    turned = jnp.concatenate(
        [first * cos_heads - second * sin_heads, second * cos_heads + first * sin_heads], axis=-1
    )
    return turned.reshape(shape)


def gated_units(values):
    units = values.shape[-1] // 2
    return jax.nn.gelu(values[..., :units], approximate=False) * values[..., units:]


def block_scores(query_heads, key_block, query_segments, segment_block, heads):
    batch, block, width = key_block.shape
    key_heads = key_block.reshape(batch, block, heads, width // heads)
    raw = jnp.einsum("bqhd,bkhd->bhqk", query_heads, key_heads, preferred_element_type=jnp.float32)
    allowed = query_segments[:, None, :, None] == segment_block[:, None, None, :]
    return jnp.where(allowed, raw, masked_score)


def attention_forward(queries, key_all, value_all, query_segments, key_segments, heads):
    batch, rows, width = queries.shape
    size = width // heads
    length = key_all.shape[1]
    block = min(512, length)
    count = length // block
    query_heads = queries.reshape(batch, rows, heads, size)

    def take(index):
        start = index * block
        return (
            lax.dynamic_slice_in_dim(key_all, start, block, 1),
            lax.dynamic_slice_in_dim(value_all, start, block, 1),
            lax.dynamic_slice_in_dim(key_segments, start, block, 1),
        )

    def stats_step(carry, index):
        running, total = carry
        key_block, value_block, segment_block = take(index)
        scores = block_scores(query_heads, key_block, query_segments, segment_block, heads)
        newest = jnp.maximum(running, jnp.max(scores, axis=-1))
        total = total * jnp.exp(running - newest) + jnp.sum(
            jnp.exp(scores - newest[..., None]), axis=-1
        )
        return ((newest, total), None)

    start_max = jnp.full((batch, heads, rows), masked_score, jnp.float32)
    start_total = jnp.zeros((batch, heads, rows), jnp.float32)
    (maximum, total), unused = lax.scan(stats_step, (start_max, start_total), jnp.arange(count))

    def value_step(carry, index):
        key_block, value_block, segment_block = take(index)
        scores = block_scores(query_heads, key_block, query_segments, segment_block, heads)
        weights = (jnp.exp(scores - maximum[..., None]) / total[..., None]).astype(jnp.bfloat16)
        value_heads = value_block.reshape(batch, block, heads, size)
        return (
            carry
            + jnp.einsum(
                "bhqk,bkhd->bqhd", weights, value_heads, preferred_element_type=jnp.float32
            ),
            None,
        )

    attended, unused = lax.scan(
        value_step, jnp.zeros((batch, rows, heads, size), jnp.float32), jnp.arange(count)
    )
    return (attended.reshape(batch, rows, width), maximum, total)


def attention_backward(
    queries, key_all, value_all, query_segments, key_segments, grad_attended, maximum, total, heads
):
    batch, rows, width = queries.shape
    size = width // heads
    length = key_all.shape[1]
    block = min(512, length)
    count = length // block
    query_heads = queries.reshape(batch, rows, heads, size)
    grad_heads = grad_attended.reshape(batch, rows, heads, size)

    def probs_block(index):
        start = index * block
        key_block = lax.dynamic_slice_in_dim(key_all, start, block, 1)
        value_block = lax.dynamic_slice_in_dim(value_all, start, block, 1)
        segment_block = lax.dynamic_slice_in_dim(key_segments, start, block, 1)
        scores = block_scores(query_heads, key_block, query_segments, segment_block, heads)
        probs = jnp.exp(scores - maximum[..., None]) / total[..., None]
        value_heads = value_block.reshape(batch, block, heads, size)
        grad_probs = jnp.einsum(
            "bqhd,bkhd->bhqk", grad_heads, value_heads, preferred_element_type=jnp.float32
        )
        return (key_block, probs, grad_probs)

    def delta_step(carry, index):
        key_block, probs, grad_probs = probs_block(index)
        return (carry + jnp.sum(probs * grad_probs, axis=-1), None)

    delta, unused = lax.scan(
        delta_step, jnp.zeros((batch, heads, rows), jnp.float32), jnp.arange(count)
    )

    def grad_step(carry, index):
        grad_query, grad_keys, grad_values = carry
        key_block, probs, grad_probs = probs_block(index)
        grad_scores = (probs * (grad_probs - delta[..., None])).astype(jnp.bfloat16)
        key_heads = key_block.reshape(batch, block, heads, size)
        grad_query = grad_query + jnp.einsum(
            "bhqk,bkhd->bqhd", grad_scores, key_heads, preferred_element_type=jnp.float32
        )
        weights = probs.astype(jnp.bfloat16)
        key_part = jnp.einsum(
            "bhqk,bqhd->bkhd", grad_scores, query_heads, preferred_element_type=jnp.float32
        )
        value_part = jnp.einsum(
            "bhqk,bqhd->bkhd", weights, grad_heads, preferred_element_type=jnp.float32
        )
        grad_keys = lax.dynamic_update_slice_in_dim(
            grad_keys, key_part.reshape(batch, block, width), index * block, 1
        )
        grad_values = lax.dynamic_update_slice_in_dim(
            grad_values, value_part.reshape(batch, block, width), index * block, 1
        )
        return ((grad_query, grad_keys, grad_values), None)

    start = (
        jnp.zeros((batch, rows, heads, size), jnp.float32),
        jnp.zeros((batch, length, width), jnp.float32),
        jnp.zeros((batch, length, width), jnp.float32),
    )
    (grad_query, grad_keys, grad_values), unused = lax.scan(grad_step, start, jnp.arange(count))
    return (grad_query.reshape(batch, rows, width), grad_keys, grad_values, delta)


def layer_pass(rows, query_segments, key_segments, cotangent, weights, cosine, sine):
    w_qkv, w_attn_out, w_in, w_mlp_out, gain_attn, gain_mlp = weights
    heads = HEADS
    width = rows.shape[-1]
    scale = (width // heads) ** (-0.5)
    rows_wide = rows.astype(jnp.float32)
    normed, norm_back = jax.vjp(norm_scale, rows_wide, gain_attn.astype(jnp.float32))
    normed_low = normed.astype(jnp.bfloat16)
    mixed = jnp.einsum("bcd,de->bce", normed_low, w_qkv, preferred_element_type=jnp.float32)

    def turn_query(values):
        return rotate_heads(values, cosine, sine, heads) * scale

    def turn_key(values):
        return rotate_heads(values, cosine, sine, heads)

    query_wide, query_back = jax.vjp(turn_query, mixed[..., :width])
    key_wide, key_back = jax.vjp(turn_key, mixed[..., width : 2 * width])
    queries = query_wide.astype(jnp.bfloat16)
    key_local = key_wide.astype(jnp.bfloat16)
    value_local = mixed[..., 2 * width :].astype(jnp.bfloat16)
    key_all, value_all = (
        lax.all_gather(key_local, "ctx", axis=1, tiled=True),
        lax.all_gather(value_local, "ctx", axis=1, tiled=True),
    )
    attended_wide, maximum, total = attention_forward(
        queries, key_all, value_all, query_segments, key_segments, heads
    )
    attended = attended_wide.astype(jnp.bfloat16)
    residual = rows_wide + jnp.einsum(
        "bcd,de->bce", attended, w_attn_out, preferred_element_type=jnp.float32
    )
    normed_mlp, norm_mlp_back = jax.vjp(norm_scale, residual, gain_mlp.astype(jnp.float32))
    normed_mlp_low = normed_mlp.astype(jnp.bfloat16)
    inner = jnp.einsum("bcd,de->bce", normed_mlp_low, w_in, preferred_element_type=jnp.float32)
    activated_wide, gated_back = jax.vjp(gated_units, inner)
    activated = activated_wide.astype(jnp.bfloat16)
    branch = jnp.einsum("bcf,fd->bcd", activated, w_mlp_out, preferred_element_type=jnp.float32)
    output = (residual + branch).astype(jnp.bfloat16)
    grad_w_mlp_out = jnp.einsum(
        "bcf,bcd->fd", activated, cotangent, preferred_element_type=jnp.float32
    )
    grad_activated = jnp.einsum(
        "bcd,fd->bcf", cotangent, w_mlp_out, preferred_element_type=jnp.float32
    )
    (grad_inner_wide,) = gated_back(grad_activated)
    grad_inner = grad_inner_wide.astype(jnp.bfloat16)
    grad_w_in = jnp.einsum(
        "bcd,bce->de", normed_mlp_low, grad_inner, preferred_element_type=jnp.float32
    )
    grad_normed_mlp = jnp.einsum(
        "bce,de->bcd", grad_inner, w_in, preferred_element_type=jnp.float32
    )
    grad_residual_part, grad_gain_mlp = norm_mlp_back(grad_normed_mlp)
    grad_residual = cotangent.astype(jnp.float32) + grad_residual_part
    grad_residual_low = grad_residual.astype(jnp.bfloat16)
    grad_w_attn_out = jnp.einsum(
        "bcd,bce->de", attended, grad_residual_low, preferred_element_type=jnp.float32
    )
    grad_attended = jnp.einsum(
        "bce,de->bcd", grad_residual_low, w_attn_out, preferred_element_type=jnp.float32
    ).astype(jnp.bfloat16)
    grad_query, grad_keys, grad_values, delta = attention_backward(
        queries,
        key_all,
        value_all,
        query_segments,
        key_segments,
        grad_attended,
        maximum,
        total,
        heads,
    )
    grad_key_local, grad_value_local = (
        lax.psum_scatter(
            grad_keys.astype(jnp.bfloat16), "ctx", scatter_dimension=1, tiled=True
        ).astype(jnp.float32),
        lax.psum_scatter(
            grad_values.astype(jnp.bfloat16), "ctx", scatter_dimension=1, tiled=True
        ).astype(jnp.float32),
    )
    (grad_query_raw,) = query_back(grad_query)
    (grad_key_raw,) = key_back(grad_key_local)
    grad_mixed = jnp.concatenate([grad_query_raw, grad_key_raw, grad_value_local], axis=-1).astype(
        jnp.bfloat16
    )
    grad_w_qkv = jnp.einsum(
        "bcd,bce->de", normed_low, grad_mixed, preferred_element_type=jnp.float32
    )
    grad_normed = jnp.einsum("bce,de->bcd", grad_mixed, w_qkv, preferred_element_type=jnp.float32)
    grad_rows_part, grad_gain_attn = norm_back(grad_normed)
    input_grad = grad_residual + grad_rows_part
    gradients = (
        grad_w_qkv,
        grad_w_attn_out,
        grad_w_in,
        grad_w_mlp_out,
        grad_gain_attn,
        grad_gain_mlp,
    )
    return (output, input_grad, gradients)


def on_device(
    hidden, segment_ids, cotangent, w_qkv, w_attn_out, w_in, w_mlp_out, gain_attn, gain_mlp
):
    shard_rows = hidden.shape[1]
    positions = lax.axis_index("ctx") * shard_rows + jnp.arange(shard_rows, dtype=jnp.int32)
    cosine, sine = rope_tables(positions, hidden.shape[2] // HEADS)
    key_segments = lax.all_gather(segment_ids, "ctx", axis=1, tiled=True)
    local_weights = (w_qkv, w_attn_out, w_in, w_mlp_out, gain_attn, gain_mlp)
    fsdp_size = lax.axis_size("fsdp")
    totals = tuple(
        (
            jnp.zeros((piece.shape[0] * fsdp_size,) + piece.shape[1:], jnp.float32)
            for piece in local_weights
        )
    )
    group = hidden.shape[0] // MICRO
    outputs = []
    input_grads = []
    for micro in range(MICRO):
        full_weights = (
            lax.all_gather(local_weights[0], "fsdp", axis=0, tiled=True),
            lax.all_gather(local_weights[1], "fsdp", axis=0, tiled=True),
            lax.all_gather(local_weights[2], "fsdp", axis=0, tiled=True),
            lax.all_gather(local_weights[3], "fsdp", axis=0, tiled=True),
            lax.all_gather(local_weights[4], "fsdp", axis=0, tiled=True),
            lax.all_gather(local_weights[5], "fsdp", axis=0, tiled=True),
        )
        lower = micro * group
        upper = lower + group
        output, input_grad, gradients = layer_pass(
            hidden[lower:upper],
            segment_ids[lower:upper],
            key_segments[lower:upper],
            cotangent[lower:upper],
            full_weights,
            cosine,
            sine,
        )
        totals = tuple((before + extra for before, extra in zip(totals, gradients)))
        outputs.append(output)
        input_grads.append(input_grad)
    shards = jax.tree.map(
        lambda part: part.astype(jnp.float32),
        lax.psum_scatter(shortened(totals), "fsdp", scatter_dimension=0, tiled=True),
    )
    summed = jax.tree.map(lambda part: part.astype(jnp.float32), lax.psum(shortened(shards), "ctx"))
    return (
        jnp.concatenate(outputs, axis=0),
        jnp.concatenate(input_grads, axis=0),
        summed[0],
        summed[1],
        summed[2],
        summed[3],
        summed[4],
        summed[5],
    )


def solution(mesh):
    in_specs = (
        P("fsdp", "ctx", None),
        P("fsdp", "ctx"),
        P("fsdp", "ctx", None),
        P("fsdp", None),
        P("fsdp", None),
        P("fsdp", None),
        P("fsdp", None),
        P("fsdp"),
        P("fsdp"),
    )
    out_specs = (
        P("fsdp", "ctx", None),
        P("fsdp", "ctx", None),
        P("fsdp", None),
        P("fsdp", None),
        P("fsdp", None),
        P("fsdp", None),
        P("fsdp"),
        P("fsdp"),
    )
    return jax.shard_map(
        on_device, mesh=mesh, in_specs=in_specs, out_specs=out_specs, check_vma=False
    )
```

profile of v0, /device:TPU:0, one launch (start us, length us, event | category | flops | bytes accessed | tf_op | source)
XLA Modules:
  0.0 1262.6 jit_solution(18199181610584061792)
XLA Ops:
  8.0 6.0 all-gather
  15.8 42.9 %all-gather.11.cloned.1.call-done = bf16[1024,3072]{1,0:T(8,128)(2,1)} async-done(((bf16[256,3072]{1,0:T(8,128)(2,1)}), bf16[1024,3072]{1,0:T(8,128)(2,1)}) %all-gather.11.cloned.1.call-update) | async-done | bytes 6291472 | tf_op jit(solution)/shard_map/all_gather | solution.py:293
  83.8 20.6 %all_gather.42 = s32[2,1024]{1,0:T(2,128)S(1)} all-gather(s32[2,128]{1,0:T(2,128)S(1)} %copy-done.115), channel_id=1, replica_groups=mesh['ctx'=8,'fsdp'=4] {'ctx'}, dimensions={1}, use_global_device_ids=true | all-gather | bytes 9216 | tf_op jit(solution)/shard_map/all_gather | solution.py:279
  104.5 5.6 all-gather.1
  110.2 19.2 %all-gather.25.cloned.1.call-done = bf16[1,1024,1024]{1,2,0:T(8,128)(2,1)} async-done(((bf16[1,128,1024]{1,2,0:T(8,128)(2,1)}), bf16[1,1024,1024]{1,2,0:T(8,128)(2,1)}) %all-gather.25.cloned.1.call-update) | async-done | bytes 2097168 | tf_op jit(solution)/shard_map/all_gather | solution.py:192
  129.4 17.1 %while.102 = (s32[]{:T(128)}, f32[1,16,128]{2,1,0:T(8,128)S(1)}, f32[1,16,128]{2,1,0:T(8,128)S(1)}, s32[1,128]{1,0:T(1,128)S(1)}, s32[2]{0:T(128)S(1)}, /*index=...) while((s32[]{:T(128)}, f32[1,16,128]{2,1,0:T(8,128)S(1)}, ...), condition=%wide.region_15.16_spmd.clone, body=%wide.region_12.0_spmd.clone.sunk | while | flops 139536384 | bytes 12106442 | solution.py:85
  146.5 33.1 %all-gather.23.cloned.1.call-done = bf16[1,1024,1024]{2,1,0:T(8,128)(2,1)} async-done(((bf16[1,128,1024]{2,1,0:T(8,128)(2,1)}), bf16[1,1024,1024]{2,1,0:T(8,128)(2,1)}) %all-gather.23.cloned.1.call-update) | async-done | bytes 2097168 | tf_op jit(solution)/shard_map/all_gather | solution.py:193
  183.5 16.4 %while.103 = (s32[]{:T(128)}, f32[1,128,16,64]{1,3,2,0:T(8,128)}, s32[2]{0:T(128)S(1)}, bf16[1,1024,1024]{1,2,0:T(8,128)(2,1)}, s32[1,128]{1,0:T(1,128)S(1)}, /*...) while((s32[]{:T(128)}, f32[1,128,16,64]{1,3,2,0:T(8,128)}, ...), condition=%wide.region_17.18_spmd.clone, body=%wide.region_16.17_spmd.clone.sunk | while | flops 272957440 | bytes 7756505 | solution.py:100
  187.7 4.0 fusion.289
  195.9 4.1 fusion.289
  201.8 27.6 %all-gather.13.cloned.1.call-done = bf16[1,1024,1024]{2,1,0:T(8,128)(2,1)} async-done(((bf16[1,128,1024]{2,1,0:T(8,128)(2,1)}), bf16[1,1024,1024]{2,1,0:T(8,128)(2,1)}) %all-gather.13.cloned.1.call-update) | async-done | bytes 2097168 | tf_op jit(solution)/shard_map/all_gather | solution.py:193
  233.3 47.6 %all-gather.15.cloned.1.call-done = bf16[1,1024,1024]{1,2,0:T(8,128)(2,1)} async-done(((bf16[1,128,1024]{1,2,0:T(8,128)(2,1)}), bf16[1,1024,1024]{1,2,0:T(8,128)(2,1)}) %all-gather.15.cloned.1.call-update) | async-done | bytes 2097168 | tf_op jit(solution)/shard_map/all_gather | solution.py:192
  280.9 17.5 %while.100 = (s32[]{:T(128)}, f32[1,16,128]{2,1,0:T(8,128)S(1)}, f32[1,16,128]{2,1,0:T(8,128)S(1)}, s32[1,128]{1,0:T(1,128)S(1)}, s32[2]{0:T(128)S(1)}, /*index=...) while((s32[]{:T(128)}, f32[1,16,128]{2,1,0:T(8,128)S(1)}, ...), condition=%wide.region_5.6_spmd.clone, body=%wide.region_2.5_spmd.clone.sunk | while | flops 139536384 | bytes 12106442 | solution.py:85
  298.4 17.4 %while.101 = (s32[]{:T(128)}, f32[1,128,16,64]{1,3,2,0:T(8,128)}, s32[2]{0:T(128)S(1)}, bf16[1,1024,1024]{1,2,0:T(8,128)(2,1)}, s32[1,128]{1,0:T(1,128)S(1)}, /*...) while((s32[]{:T(128)}, f32[1,128,16,64]{1,3,2,0:T(8,128)}, ...), condition=%wide.region_7.8_spmd.clone, body=%wide.region_6.7_spmd.clone.sunk | while | flops 272957440 | bytes 7756505 | solution.py:100
  302.8 4.0 fusion.283
  311.2 4.5 fusion.283
  321.7 54.7 %all-gather.19.cloned.1.call-done = bf16[1024,5248]{1,0:T(8,128)(2,1)} async-done(((bf16[256,5248]{1,0:T(8,128)(2,1)}), bf16[1024,5248]{1,0:T(8,128)(2,1)}) %all-gather.19.cloned.1.call-update) | async-done | bytes 10747920 | tf_op jit(solution)/shard_map/all_gather | solution.py:295
  376.4 7.5 convolution_bitcast_fusion.2
  383.8 35.3 %all-gather.21.cloned.1.call-done = bf16[2624,1024]{1,0:T(8,128)(2,1)} async-done(((bf16[656,1024]{1,0:T(8,128)(2,1)}), bf16[2624,1024]{1,0:T(8,128)(2,1)}) %all-gather.21.cloned.1.call-update) | async-done | bytes 5373968 | tf_op jit(solution)/shard_map/all_gather | solution.py:296
  419.2 8.1 fusion.114
  430.9 5.5 fusion.115
  438.1 5.5 fusion.137
  443.6 6.4 fusion.111
  454.8 10.5 while.106
  468.5 28.0 %while.107 = (s32[]{:T(128)}, f32[1,128,16,64]{1,3,2,0:T(8,128)}, bf16[1,1024,1024]{1,2,0:T(8,128)(2,1)}, bf16[1,1024,1024]{1,2,0:T(8,128)(2,1)}, s32[2]{0:T(128...) while((s32[]{:T(128)}, f32[1,128,16,64]{1,3,2,0:T(8,128)}, ...), condition=%wide.region_37.38_spmd.clone, body=%wide.region_36.37_spmd.clone.sunk | while | flops 678756352 | bytes 129137728 | solution.py:166
  496.5 10.7 copy.107
  507.2 4.4 copy.117
  514.3 11.2 while.104
  528.6 32.8 %while.105 = (s32[]{:T(128)}, f32[1,128,16,64]{1,3,2,0:T(8,128)}, bf16[1,1024,1024]{1,2,0:T(8,128)(2,1)}, bf16[1,1024,1024]{1,2,0:T(8,128)(2,1)}, s32[2]{0:T(128...) while((s32[]{:T(128)}, f32[1,128,16,64]{1,3,2,0:T(8,128)}, ...), condition=%wide.region_26.27_spmd.clone, body=%wide.region_25.26_spmd.clone.sunk | while | flops 678756352 | bytes 103971808 | solution.py:166
  561.5 10.8 copy.101
  572.3 4.4 copy.120
  578.3 7.5 copy.105
  585.8 4.3 copy.118
  591.7 7.5 copy.103
  599.2 4.4 copy.119
  610.2 4.0 add_convert_fusion.2
  617.2 32.4 %reduce-scatter.25.cloned.1.call-done = bf16[128,1024]{1,0:T(8,128)(2,1)} async-done(((bf16[1024,1024]{1,0:T(8,128)(2,1)}), bf16[128,1024]{1,0:T(8,128)(2,1)}) %reduce-scatter.25.cloned.1.call-update) | async-done | bytes 262160
  651.4 69.2 %reduce-scatter.29.cloned.1.call-done = bf16[128,1024]{1,0:T(8,128)(2,1)} async-done(((bf16[1024,1024]{1,0:T(8,128)(2,1)}), bf16[128,1024]{1,0:T(8,128)(2,1)}) %reduce-scatter.29.cloned.1.call-update) | async-done | bytes 262160
  723.9 67.0 %reduce-scatter.27.cloned.1.call-done = bf16[128,1024]{1,0:T(8,128)(2,1)} async-done(((bf16[1024,1024]{1,0:T(8,128)(2,1)}), bf16[128,1024]{1,0:T(8,128)(2,1)}) %reduce-scatter.27.cloned.1.call-update) | async-done | bytes 262160
  796.9 4.8 add_convert_fusion.1
  802.8 11.0 fusion.139
  813.8 12.7 %add_convert_fusion = bf16[1024,5248]{1,0:T(8,128)(2,1)} fusion(f32[1024,5248]{1,0:T(8,128)} %fusion.139, f32[1,128,2624]{2,1,0:T(8,128)S(1)} %copy-done.29, f32[1,128,2624]{2,1,0:T(8,128)} %get-tuple-element.1168, f32[1,128,1024]{2,1,0:T(8,128)S(1)} %copy-done.22, f32[128]{0:T(128)S(1)} %copy-done.114, f32[128]{0:T(128)S(1)} %copy-done.110, ...), kind=kOutput, calls=%fused_computation.120 | convolution fusion | flops 1388347392 | bytes 35460096 | tf_op jit(solution)/shard_map/bcd,bce->de/dot_general | solution.py:217
  826.6 52.7 %reduce-scatter.23.cloned.1.call-done = bf16[656,1024]{1,0:T(8,128)(2,1)} async-done(((bf16[2624,1024]{1,0:T(8,128)(2,1)}), bf16[656,1024]{1,0:T(8,128)(2,1)}) %reduce-scatter.23.cloned.1.call-update) | async-done | bytes 1343504 | tf_op jit(solution)/shard_map/reduce_scatter | solution.py:316
  879.4 60.8 %reduce-scatter.17.cloned.1.call-done = bf16[256,3072]{1,0:T(8,128)(2,1)} async-done(((bf16[1024,3072]{1,0:T(8,128)(2,1)}), bf16[256,3072]{1,0:T(8,128)(2,1)}) %reduce-scatter.17.cloned.1.call-update) | async-done | bytes 1572880 | tf_op jit(solution)/shard_map/reduce_scatter | solution.py:316
  940.2 89.7 %reduce-scatter.21.cloned.1.call-done = bf16[256,5248]{1,0:T(8,128)(2,1)} async-done(((bf16[1024,5248]{1,0:T(8,128)(2,1)}), bf16[256,5248]{1,0:T(8,128)(2,1)}) %reduce-scatter.21.cloned.1.call-update) | async-done | bytes 2686992 | tf_op jit(solution)/shard_map/reduce_scatter | solution.py:316
  1045.4 6.1 all-reduce.16
  1051.6 22.6 %all-reduce.14 = (bf16[256]{0:T(256)(128)(2,1)S(1)}, bf16[256]{0:T(256)(128)(2,1)S(1)}) all-reduce(bf16[256]{0:T(256)(128)(2,1)S(1)} %dynamic-slice.1, bf16[256]{0:T(256)(128)(2,1)S(1)} %dynamic-slice.3), channel_id=1, replica_groups=mesh['ctx'=8,'fsdp'=4] {'ctx'}, use_global_device_ids=true, to_apply=%region_53.54 | all-reduce | flops 512 | bytes 2048 | tf_op jit(solution)/shard_map/psum | solution.py:318
  1077.0 169.4 %all-reduce.19.cloned.1.call-done = (bf16[256,3072]{1,0:T(8,128)(2,1)}, bf16[256,1024]{1,0:T(8,128)(2,1)}, bf16[256,5248]{1,0:T(8,128)(2,1)}, bf16[656,1024]{1,0:T(8,128)(2,1)}) async-done(((bf16[256,3072]{1,0:T(8,128)(2,1)}, bf16[256,1024]{1,0:T(8,128)(2,1)}, bf16[256,5248]{1,0:T(8,128)(2,1)}, bf16[656,1024]{1,0:T(8,128)(2,1)}), (bf16[256,3072]{1,0:T(8,128)(2,1)}, bf16[256,1024]{1,0:T(8,128)(2,1)}, ...) | async-done | bytes 6127632 | tf_op jit(solution)/shard_map/psum | solution.py:318
  (583 shorter events, 235.6 us)
Async XLA Ops:
  7.2 51.5 %all-gather.11.cloned.1.call-start = ((), (), s32[]{:S(2)}) async-start(), calls=%async_computation.8 | async-start | bytes 7864320 | tf_op jit(solution)/shard_map/all_gather | solution.py:293
  7.9 121.5 %all-gather.25.cloned.1.call-start = ((), (), s32[]{:S(2)}) async-start(), calls=%async_computation.15 | async-start | bytes 2359296 | tf_op jit(solution)/shard_map/all_gather | solution.py:192
  14.0 49.7 %copy-start.78 = (f32[4,1,256]{2,1,0:T(1,128)}, f32[4,1,256]{2,1,0:T(1,128)S(1)}, u32[]{:S(2)}) copy-start(f32[4,1,256]{2,1,0:T(1,128)S(1)} %convert_element_type.286) | copy-start | bytes 12292
  14.2 48.3 %copy-start.97 = (f32[128]{0:T(128)}, f32[128]{0:T(128)S(1)}, u32[]{:S(2)}) copy-start(f32[128]{0:T(128)S(1)} %get-tuple-element.1245) | copy-start | bytes 1540
  14.2 49.5 %copy-start.101 = (f32[128]{0:T(128)}, f32[128]{0:T(128)S(1)}, u32[]{:S(2)}) copy-start(f32[128]{0:T(128)S(1)} %get-tuple-element.1244) | copy-start | bytes 1540
  14.5 48.0 %copy-start.122 = (f32[128]{0:T(128)}, f32[128]{0:T(128)S(1)}, u32[]{:S(2)}) copy-start(f32[128]{0:T(128)S(1)} %get-tuple-element.978) | copy-start | bytes 1540
  15.1 48.6 %copy-start.107 = (f32[128]{0:T(128)}, f32[128]{0:T(128)S(1)}, u32[]{:S(2)}) copy-start(f32[128]{0:T(128)S(1)} %fusion.145) | copy-start | bytes 1540
  15.1 47.5 %copy-start.103 = (f32[128]{0:T(128)}, f32[128]{0:T(128)S(1)}, u32[]{:S(2)}) copy-start(f32[128]{0:T(128)S(1)} %fusion.143) | copy-start | bytes 1540
  15.8 59.2 %copy-start.94 = (f32[128,32]{0,1:T(8,128)}, f32[128,32]{0,1:T(8,128)S(1)}, u32[]{:S(2)}) copy-start(f32[128,32]{0,1:T(8,128)S(1)} %get-tuple-element.1234) | copy-start | bytes 49156
  78.1 101.5 %all-gather.23.cloned.1.call-start = ((), (), s32[]{:S(2)}) async-start(), calls=%async_computation.14 | async-start | bytes 2359296 | tf_op jit(solution)/shard_map/all_gather | solution.py:193
  80.0 149.4 %all-gather.13.cloned.1.call-start = ((), (), s32[]{:S(2)}) async-start(), calls=%async_computation.9 | async-start | bytes 2359296 | tf_op jit(solution)/shard_map/all_gather | solution.py:193
  80.8 200.1 %all-gather.15.cloned.1.call-start = ((), (), s32[]{:S(2)}) async-start(), calls=%async_computation.10 | async-start | bytes 2359296 | tf_op jit(solution)/shard_map/all_gather | solution.py:192
  81.6 235.6 %all-gather.17.cloned.1.call-start = ((), (), s32[]{:S(2)}) async-start(), calls=%async_computation.11 | async-start | bytes 2621440 | tf_op jit(solution)/shard_map/all_gather | solution.py:294
  82.2 22.2 %copy-start.125 = (bf16[256]{0:T(256)(128)(2,1)S(1)}, bf16[256]{0:T(256)(128)(2,1)}, u32[]{:S(2)}) copy-start(bf16[256]{0:T(256)(128)(2,1)} %param.33) | copy-start | bytes 1540
  82.2 27.9 %copy-start.71 = (f32[1,128,16,32]{1,3,2,0:T(8,128)S(1)}, f32[1,128,16,32]{1,3,2,0:T(8,128)}, u32[]{:S(2)}) copy-start(f32[1,128,16,32]{1,3,2,0:T(8,128)} %get-tuple-element.1223) | copy-start | bytes 786436
  82.2 294.1 %all-gather.19.cloned.1.call-start = ((), (), s32[]{:S(2)}) async-start(), calls=%async_computation.12 | async-start | bytes 13434880 | tf_op jit(solution)/shard_map/all_gather | solution.py:295
  83.0 27.2 %copy-start.69 = (f32[1,128,16,32]{1,3,2,0:T(8,128)S(1)}, f32[1,128,16,32]{1,3,2,0:T(8,128)}, u32[]{:S(2)}) copy-start(f32[1,128,16,32]{1,3,2,0:T(8,128)} %get-tuple-element.1204) | copy-start | bytes 786436
  83.0 27.2 %copy-start.70 = (f32[1,128,16,32]{1,3,2,0:T(8,128)S(1)}, f32[1,128,16,32]{1,3,2,0:T(8,128)}, u32[]{:S(2)}) copy-start(f32[1,128,16,32]{1,3,2,0:T(8,128)} %get-tuple-element.1205) | copy-start | bytes 786436
  83.0 336.1 %all-gather.21.cloned.1.call-start = ((), (), s32[]{:S(2)}) async-start(), calls=%async_computation.13 | async-start | bytes 6717440 | tf_op jit(solution)/shard_map/all_gather | solution.py:296
  83.8 531.8 %reduce-scatter.31.cloned.1.call-start = ((), (), s32[]{:S(2)}) async-start(), calls=%async_computation.23 | async-start | bytes 2359296
  110.1 339.9 %copy-start.80 = (f32[4,1,256]{2,1,0:T(1,128)}, f32[4,1,256]{2,1,0:T(1,128)S(1)}, u32[]{:S(2)}) copy-start(f32[4,1,256]{2,1,0:T(1,128)S(1)} %convert_element_type.287) | copy-start | bytes 12292
  146.5 37.0 %copy-start.5 = (bf16[1,1024,1024]{1,2,0:T(8,128)(2,1)S(1)}, bf16[1,1024,1024]{1,2,0:T(8,128)(2,1)}, u32[]{:S(2)}) copy-start(bf16[1,1024,1024]{1,2,0:T(8,128)(2,1)} %get-tuple-element.2186) | copy-start | bytes 6291460
  319.9 130.1 %copy-start.109 = (f32[128]{0:T(128)}, f32[128]{0:T(128)S(1)}, u32[]{:S(2)}) copy-start(f32[128]{0:T(128)S(1)} %broadcast_multiply_fusion.2) | copy-start | bytes 1540
  320.7 129.3 %copy-start.99 = (f32[128]{0:T(128)}, f32[128]{0:T(128)S(1)}, u32[]{:S(2)}) copy-start(f32[128]{0:T(128)S(1)} %broadcast_multiply_fusion.4) | copy-start | bytes 1540
  321.7 128.3 %copy-start.113 = (f32[128]{0:T(128)}, f32[128]{0:T(128)S(1)}, u32[]{:S(2)}) copy-start(f32[128]{0:T(128)S(1)} %fusion.146) | copy-start | bytes 1540
  321.7 128.3 %copy-start.105 = (f32[128]{0:T(128)}, f32[128]{0:T(128)S(1)}, u32[]{:S(2)}) copy-start(f32[128]{0:T(128)S(1)} %fusion.144) | copy-start | bytes 1540
  376.4 42.8 %copy-start.47 = (bf16[2,128,1024]{2,1,0:T(8,128)(2,1)S(1)}, bf16[2,128,1024]{2,1,0:T(8,128)(2,1)}, u32[]{:S(2)}) copy-start(bf16[2,128,1024]{2,1,0:T(8,128)(2,1)} %param.27) | copy-start | bytes 1572868
  419.2 9.8 copy-start.4
  428.9 9.2 copy-start.28
  511.6 138.0 %reduce-scatter.25.cloned.1.call-start = ((), (), s32[]{:S(2)}) async-start(), calls=%async_computation.20 | async-start | bytes 2359296
  576.7 143.9 %reduce-scatter.29.cloned.1.call-start = ((), (), s32[]{:S(2)}) async-start(), calls=%async_computation.22 | async-start | bytes 2359296
  590.1 200.8 %reduce-scatter.27.cloned.1.call-start = ((), (), s32[]{:S(2)}) async-start(), calls=%async_computation.21 | async-start | bytes 2359296
  603.6 223.0 %reduce-scatter.19.cloned.1.call-start = ((), (), s32[]{:S(2)}) async-start(), calls=%async_computation.17 | async-start | bytes 2621440 | tf_op jit(solution)/shard_map/reduce_scatter | solution.py:316
  607.4 271.9 %reduce-scatter.23.cloned.1.call-start = ((), (), s32[]{:S(2)}) async-start(), calls=%async_computation.19 | async-start | bytes 6717440 | tf_op jit(solution)/shard_map/reduce_scatter | solution.py:316
  614.3 325.9 %reduce-scatter.17.cloned.1.call-start = ((), (), s32[]{:S(2)}) async-start(), calls=%async_computation.16 | async-start | bytes 7864320 | tf_op jit(solution)/shard_map/reduce_scatter | solution.py:316
  617.2 179.7 %copy-start.63 = (bf16[1,128,1024]{1,2,0:T(8,128)(2,1)}, bf16[1,128,1024]{1,2,0:T(8,128)(2,1)S(1)}, u32[]{:S(2)}) copy-start(bf16[1,128,1024]{1,2,0:T(8,128)(2,1)S(1)} %copy.108) | copy-start | bytes 786436
  721.8 71.3 %copy-start.95 = (f32[128,32]{0,1:T(8,128)S(1)}, f32[128,32]{0,1:T(8,128)}, u32[]{:S(2)}) copy-start(f32[128,32]{0,1:T(8,128)} %copy-done.94) | copy-start | bytes 49156
  721.8 71.3 %copy-start.96 = (f32[128,32]{0,1:T(8,128)S(1)}, f32[128,32]{0,1:T(8,128)}, u32[]{:S(2)}) copy-start(f32[128,32]{0,1:T(8,128)} %get-tuple-element.1235) | copy-start | bytes 49156
  801.7 12.1 copy-start.22
  801.7 12.1 copy-start.29
  801.8 12.0 copy-start.110
  801.8 12.0 copy-start.114
  801.8 228.1 %reduce-scatter.21.cloned.1.call-start = ((), (), s32[]{:S(2)}) async-start(), calls=%async_computation.18 | async-start | bytes 13434880 | tf_op jit(solution)/shard_map/reduce_scatter | solution.py:316
  826.6 419.8 %all-reduce.19.cloned.1.call-start = ((), (), s32[]{:S(2)}) async-start(), calls=%async_computation.24 | async-start | bytes 12255232 | tf_op jit(solution)/shard_map/psum | solution.py:318
  1044.7 30.7 %copy-start.51 = (f32[1,128,1024]{2,1,0:T(8,128)S(1)}, f32[1,128,1024]{2,1,0:T(8,128)}, u32[]{:S(2)}) copy-start(f32[1,128,1024]{2,1,0:T(8,128)} %copy-done.50) | copy-start | bytes 1572868
  1044.7 30.7 %copy-start.53 = (f32[1,128,1024]{2,1,0:T(8,128)S(1)}, f32[1,128,1024]{2,1,0:T(8,128)}, u32[]{:S(2)}) copy-start(f32[1,128,1024]{2,1,0:T(8,128)} %copy-done.52) | copy-start | bytes 1572868
  1044.7 30.7 %copy-start.117 = (f32[128]{0:T(128)S(1)}, f32[128]{0:T(128)}, u32[]{:S(2)}) copy-start(f32[128]{0:T(128)} %copy-done.116) | copy-start | bytes 1540
  1044.7 30.7 %copy-start.119 = (f32[128]{0:T(128)S(1)}, f32[128]{0:T(128)}, u32[]{:S(2)}) copy-start(f32[128]{0:T(128)} %copy-done.118) | copy-start | bytes 1540
  (119 other events, 289.3 us)
Sparse Core Ops, SparseCore 0:
  9.6 49.0 all-gather.10
  78.3 51.0 all-gather.24
  132.1 47.4 all-gather.22
  181.6 47.7 all-gather.12
  231.3 49.5 all-gather.14
  282.3 20.7 all-gather.16
  304.7 71.6 all-gather.18
  377.9 41.1 all-gather.20
  511.7 67.6 reduce-scatter.30
  582.8 66.8 reduce-scatter.24
  653.8 66.8 reduce-scatter.28
  724.0 66.8 reduce-scatter.26
  793.4 30.4 reduce-scatter.18
  827.1 52.2 reduce-scatter.22
  881.7 58.3 reduce-scatter.16
  942.8 86.9 reduce-scatter.20
  1035.1 211.2 all-reduce.18
where the time goes:
time: 1270 us; the launch traced here: 1260 us
  waiting for transfers between devices  804 us (63%)
  matrix products  167 us (13%)
  local copies, waits for them, and re-layouts  157 us (12%)
  blocking collectives  60.9 us (5%)
  other arithmetic  43.5 us (3%)
  between operations  16.7 us (1%)
    reduce_scatter x4, waiting for transfers between devices, on_device(): lax.psum_scatter(shortened(totals), 'fsdp', scatter_dimension=0, tiled=True)  203 us
    unnamed x21, waiting for transfers between devices  171 us
    psum x1, waiting for transfers between devices, on_device(): lax.psum(shortened(shards), 'ctx')  169 us
    unnamed x247, local copies, waits for them, and re-layouts  84.9 us
    all_gather x2, waiting for transfers between devices, layer_pass(): lax.all_gather(key_local, 'ctx', axis=1, tiled=True)  66.7 us
    all_gather x2, waiting for transfers between devices, layer_pass(): lax.all_gather(value_local, 'ctx', axis=1, tiled=True)  60.7 us
    all_gather x1, waiting for transfers between devices, on_device(): lax.all_gather(local_weights[2], 'fsdp', axis=0, tiled=True)  54.7 us
    all_gather x1, waiting for transfers between devices, on_device(): lax.all_gather(local_weights[0], 'fsdp', axis=0, tiled=True)  42.9 us
  transfers between devices with their start and end apart: 17, of which 14 were waited for; matrix products, arithmetic and copies ran while one was open for 18% of the time, Pallas kernels for 0%

commit v1 on v0

--- a/solution.py
+++ b/solution.py
@@ -8,6 +8,19 @@
 rope_base = 160000.0
 norm_eps = 1e-05
 masked_score = -1e30
+
+
+def collect(x, axis, dim):
+    ways = lax.axis_size(axis)
+    up = [(d, (d + 1) % ways) for d in range(ways)]
+    down = [(d, (d - 1) % ways) for d in range(ways)]
+    earlier, later = ([x], [x])
+    for _ in range(ways // 2):
+        earlier.append(lax.ppermute(earlier[-1], axis, up))
+    for _ in range((ways - 1) // 2):
+        later.append(lax.ppermute(later[-1], axis, down))
+    line = jnp.concatenate([*earlier[::-1], *later[1:]], axis=dim)
+    return jnp.roll(line, (lax.axis_index(axis) - ways // 2) * x.shape[dim], axis=dim)
 
 
 def shortened(value):
@@ -190,7 +203,7 @@
     value_local = mixed[..., 2 * width :].astype(jnp.bfloat16)
     key_all, value_all = (
         lax.all_gather(key_local, "ctx", axis=1, tiled=True),
-        lax.all_gather(value_local, "ctx", axis=1, tiled=True),
+        collect(value_local, "ctx", 1),
     )
     attended_wide, maximum, total = attention_forward(
         queries, key_all, value_all, query_segments, key_segments, heads

time: 1270 us -> 1210 us (0.953)
  waiting for transfers between devices: 804 us -> 687 us
  starting transfers between devices: 1.15 us -> 18.4 us
  local copies, waits for them, and re-layouts: 157 us -> 174 us
    all_gather x2, waiting for transfers between devices: 66.7 us -> 0.02 us  [layer_pass(): lax.all_gather(key_local, 'ctx', axis=1, tiled=True)]
    all_gather x2 -> x0, waiting for transfers between devices: 60.7 us -> none  [layer_pass(): lax.all_gather(value_local, 'ctx', axis=1, tiled=True)]
    ppermute x0 -> x14, waiting for transfers between devices: none -> 45.4 us  [the longest x8 28.6 us: collect(): earlier.append(lax.ppermute(earlier[-1], axis, up))]
    all_gather x1, waiting for transfers between devices: 54.7 us -> 21.8 us  [on_device(): lax.all_gather(local_weights[2], 'fsdp', axis=0, tiled=True)]
    ppermute x0 -> x14, starting transfers between devices: none -> 17.4 us  [the longest x8 12 us: collect(): earlier.append(lax.ppermute(earlier[-1], axis, up))]
    unnamed x247 -> x267, local copies, waits for them, and re-layouts: 84.9 us -> 94.1 us
    unnamed x21 -> x19, waiting for transfers between devices: 171 us -> 171 us
  transfers between devices with their start and end apart: 17 -> 29, of which waited for: 14 -> 17; matrix products, arithmetic and copies ran while one was open for 18% -> 21% of each run, Pallas kernels for 0% -> 0%
where the time goes in v1:
time: 1210 us; the launch traced here: 1200 us
  waiting for transfers between devices  687 us (57%)
  local copies, waits for them, and re-layouts  174 us (14%)
  matrix products  163 us (13%)
  blocking collectives  71.6 us (6%)
  other arithmetic  53.1 us (4%)
  starting transfers between devices  18.4 us (2%)
  between operations  16.7 us (1%)
  loops' own time  12.3 us (1%)
    reduce_scatter x4, waiting for transfers between devices, on_device(): lax.psum_scatter(shortened(totals), 'fsdp', scatter_dimension=0, tiled=True)  203 us
    unnamed x19, waiting for transfers between devices  171 us
    psum x1, waiting for transfers between devices, on_device(): lax.psum(shortened(shards), 'ctx')  169 us
    unnamed x267, local copies, waits for them, and re-layouts  94.1 us
    all_gather x1, waiting for transfers between devices, on_device(): lax.all_gather(local_weights[0], 'fsdp', axis=0, tiled=True)  41.3 us
    all_gather x1, waiting for transfers between devices, on_device(): lax.all_gather(local_weights[3], 'fsdp', axis=0, tiled=True)  35.2 us
    all_gather x1, blocking collectives, on_device(): key_segments = lax.all_gather(segment_ids, 'ctx', axis=1, tiled=True)  31.8 us
    ppermute x8, waiting for transfers between devices, collect(): earlier.append(lax.ppermute(earlier[-1], axis, up))  28.6 us
  transfers between devices with their start and end apart: 29, of which 17 were waited for; matrix products, arithmetic and copies ran while one was open for 21% of the time, Pallas kernels for 0%

profile of v1, /device:TPU:0, one launch (start us, length us, event | category | flops | bytes accessed | tf_op | source)
XLA Modules:
  0.0 1195.4 jit_solution(17024378726389370133)
XLA Ops:
  8.6 6.0 all-gather
  17.4 41.3 %all-gather.9.cloned.1.call-done = bf16[1024,3072]{1,0:T(8,128)(2,1)} async-done(((bf16[256,3072]{1,0:T(8,128)(2,1)}), bf16[1024,3072]{1,0:T(8,128)(2,1)}) %all-gather.9.cloned.1.call-update) | async-done | bytes 6291472 | tf_op jit(solution)/shard_map/all_gather | solution.py:306
  86.7 11.2 collective-permute-done.7
  97.9 4.7 collective-permute-start.11
  102.7 4.6 collective-permute-done
  107.2 9.3 collective-permute-done.8
  119.2 31.8 %all_gather.35 = s32[2,1024]{1,0:T(2,128)S(1)} all-gather(s32[2,128]{1,0:T(2,128)S(1)} %copy-done.116), channel_id=1, replica_groups=mesh['ctx'=8,'fsdp'=4] {'ctx'}, dimensions={1}, use_global_device_ids=true | all-gather | bytes 9216 | tf_op jit(solution)/shard_map/all_gather | solution.py:292
  156.1 5.1 all-gather.1
  161.4 10.8 collective-permute-done.12
  172.2 6.0 collective-permute-done.5
  203.8 4.6 fusion.65
  211.3 17.2 %while.102 = (s32[]{:T(128)}, f32[1,16,128]{2,1,0:T(8,128)S(1)}, f32[1,16,128]{2,1,0:T(8,128)S(1)}, s32[1,128]{1,0:T(1,128)S(1)}, s32[2]{0:T(128)S(1)}, /*index=...) while((s32[]{:T(128)}, f32[1,16,128]{2,1,0:T(8,128)S(1)}, ...), condition=%wide.region_15.17_spmd.clone, body=%wide.region_12.16_spmd.clone.sunk | while | flops 139536384 | bytes 12106442 | solution.py:98
  228.6 17.1 %while.103 = (s32[]{:T(128)}, f32[1,128,16,64]{1,3,2,0:T(8,128)}, s32[2]{0:T(128)S(1)}, bf16[1,1024,1024]{1,2,0:T(8,128)(2,1)}, s32[1,128]{1,0:T(1,128)S(1)}, /*...) while((s32[]{:T(128)}, f32[1,128,16,64]{1,3,2,0:T(8,128)}, ...), condition=%wide.region_17.19_spmd.clone, body=%wide.region_16.18_spmd.clone.sunk | while | flops 272957440 | bytes 7756505 | solution.py:113
  241.4 4.3 fusion.291
  247.6 17.2 %while.100 = (s32[]{:T(128)}, f32[1,16,128]{2,1,0:T(8,128)S(1)}, f32[1,16,128]{2,1,0:T(8,128)S(1)}, s32[1,128]{1,0:T(1,128)S(1)}, s32[2]{0:T(128)S(1)}, /*index=...) while((s32[]{:T(128)}, f32[1,16,128]{2,1,0:T(8,128)S(1)}, ...), condition=%wide.region_5.7_spmd.clone, body=%wide.region_2.6_spmd.clone.sunk | while | flops 139536384 | bytes 12106442 | solution.py:98
  264.8 16.7 %while.101 = (s32[]{:T(128)}, f32[1,128,16,64]{1,3,2,0:T(8,128)}, s32[2]{0:T(128)S(1)}, bf16[1,1024,1024]{1,2,0:T(8,128)(2,1)S(1)}, s32[1,128]{1,0:T(1,128)S(1)}...) while((s32[]{:T(128)}, f32[1,128,16,64]{1,3,2,0:T(8,128)}, ...), condition=%wide.region_7.9_spmd.clone, body=%wide.region_6.8_spmd.clone.sunk | while | flops 272957440 | bytes 7756505 | solution.py:113
  277.1 4.1 fusion.285
  286.7 21.8 %all-gather.15.cloned.1.call-done = bf16[1024,5248]{1,0:T(8,128)(2,1)} async-done(((bf16[256,5248]{1,0:T(8,128)(2,1)}), bf16[1024,5248]{1,0:T(8,128)(2,1)}) %all-gather.15.cloned.1.call-update) | async-done | bytes 10747920 | tf_op jit(solution)/shard_map/all_gather | solution.py:308
  308.5 7.5 convolution_bitcast_fusion.2
  316.0 35.2 %all-gather.17.cloned.1.call-done = bf16[2624,1024]{1,0:T(8,128)(2,1)} async-done(((bf16[656,1024]{1,0:T(8,128)(2,1)}), bf16[2624,1024]{1,0:T(8,128)(2,1)}) %all-gather.17.cloned.1.call-update) | async-done | bytes 5373968 | tf_op jit(solution)/shard_map/all_gather | solution.py:309
  351.2 7.0 fusion.116
  362.1 5.3 fusion.117
  372.7 5.8 fusion.113
  382.4 11.0 while.106
  396.5 32.7 %while.107 = (s32[]{:T(128)}, f32[1,128,16,64]{1,3,2,0:T(8,128)}, bf16[1,1024,1024]{1,2,0:T(8,128)(2,1)}, bf16[1,1024,1024]{1,2,0:T(8,128)(2,1)}, s32[2]{0:T(128...) while((s32[]{:T(128)}, f32[1,128,16,64]{1,3,2,0:T(8,128)}, ...), condition=%wide.region_37.39_spmd.clone, body=%wide.region_36.38_spmd.clone.sunk | while | flops 678756352 | bytes 103971808 | solution.py:179
  429.2 10.7 copy.107
  439.9 4.4 copy.117
  446.9 11.4 while.104
  461.6 32.9 %while.105 = (s32[]{:T(128)}, f32[1,128,16,64]{1,3,2,0:T(8,128)}, bf16[1,1024,1024]{1,2,0:T(8,128)(2,1)}, bf16[1,1024,1024]{1,2,0:T(8,128)(2,1)}, s32[2]{0:T(128...) while((s32[]{:T(128)}, f32[1,128,16,64]{1,3,2,0:T(8,128)}, ...), condition=%wide.region_26.28_spmd.clone, body=%wide.region_25.27_spmd.clone.sunk | while | flops 678756352 | bytes 103971808 | solution.py:179
  494.5 10.8 copy.101
  505.2 4.4 copy.120
  511.2 7.5 copy.105
  518.7 4.3 copy.118
  524.7 7.5 copy.103
  532.2 4.4 copy.119
  543.2 4.0 add_convert_fusion.2
  550.2 32.5 %reduce-scatter.25.cloned.1.call-done = bf16[128,1024]{1,0:T(8,128)(2,1)} async-done(((bf16[1024,1024]{1,0:T(8,128)(2,1)}), bf16[128,1024]{1,0:T(8,128)(2,1)}) %reduce-scatter.25.cloned.1.call-update) | async-done | bytes 262160
  584.5 69.3 %reduce-scatter.29.cloned.1.call-done = bf16[128,1024]{1,0:T(8,128)(2,1)} async-done(((bf16[1024,1024]{1,0:T(8,128)(2,1)}), bf16[128,1024]{1,0:T(8,128)(2,1)}) %reduce-scatter.29.cloned.1.call-update) | async-done | bytes 262160
  657.0 67.0 %reduce-scatter.27.cloned.1.call-done = bf16[128,1024]{1,0:T(8,128)(2,1)} async-done(((bf16[1024,1024]{1,0:T(8,128)(2,1)}), bf16[128,1024]{1,0:T(8,128)(2,1)}) %reduce-scatter.27.cloned.1.call-update) | async-done | bytes 262160
  730.0 4.8 add_convert_fusion.1
  735.9 11.0 fusion.141
  746.9 12.7 %add_convert_fusion = bf16[1024,5248]{1,0:T(8,128)(2,1)} fusion(f32[1024,5248]{1,0:T(8,128)} %fusion.141, f32[1,128,2624]{2,1,0:T(8,128)S(1)} %copy-done.25, f32[1,128,2624]{2,1,0:T(8,128)} %copy-done.43, f32[1,128,1024]{2,1,0:T(8,128)S(1)} %copy-done.19, f32[128]{0:T(128)S(1)} %copy-done.115, f32[128]{0:T(128)S(1)} %copy-done.111, f32[1024]{0:T(1024)S(1)} %bitcast.795), kind=kOutput, calls=%fused_computation.120 | convolution fusion | flops 1388347392 | bytes 35460096 | tf_op jit(solution)/shard_map/bcd,bce->de/dot_general | solution.py:230
  759.7 52.7 %reduce-scatter.23.cloned.1.call-done = bf16[656,1024]{1,0:T(8,128)(2,1)} async-done(((bf16[2624,1024]{1,0:T(8,128)(2,1)}), bf16[656,1024]{1,0:T(8,128)(2,1)}) %reduce-scatter.23.cloned.1.call-update) | async-done | bytes 1343504 | tf_op jit(solution)/shard_map/reduce_scatter | solution.py:329
  812.4 60.9 %reduce-scatter.17.cloned.1.call-done = bf16[256,3072]{1,0:T(8,128)(2,1)} async-done(((bf16[1024,3072]{1,0:T(8,128)(2,1)}), bf16[256,3072]{1,0:T(8,128)(2,1)}) %reduce-scatter.17.cloned.1.call-update) | async-done | bytes 1572880 | tf_op jit(solution)/shard_map/reduce_scatter | solution.py:329
  873.3 89.7 %reduce-scatter.21.cloned.1.call-done = bf16[256,5248]{1,0:T(8,128)(2,1)} async-done(((bf16[1024,5248]{1,0:T(8,128)(2,1)}), bf16[256,5248]{1,0:T(8,128)(2,1)}) %reduce-scatter.21.cloned.1.call-update) | async-done | bytes 2686992 | tf_op jit(solution)/shard_map/reduce_scatter | solution.py:329
  978.5 6.1 all-reduce.16
  984.8 22.7 %all-reduce.14 = (bf16[256]{0:T(256)(128)(2,1)S(1)}, bf16[256]{0:T(256)(128)(2,1)S(1)}) all-reduce(bf16[256]{0:T(256)(128)(2,1)S(1)} %dynamic-slice.1, bf16[256]{0:T(256)(128)(2,1)S(1)} %dynamic-slice.3), channel_id=1, replica_groups=mesh['ctx'=8,'fsdp'=4] {'ctx'}, use_global_device_ids=true, to_apply=%region_53.55 | all-reduce | flops 512 | bytes 2048 | tf_op jit(solution)/shard_map/psum | solution.py:331
  1010.1 169.2 %all-reduce.19.cloned.1.call-done = (bf16[256,3072]{1,0:T(8,128)(2,1)}, bf16[256,1024]{1,0:T(8,128)(2,1)}, bf16[256,5248]{1,0:T(8,128)(2,1)}, bf16[656,1024]{1,0:T(8,128)(2,1)}) async-done(((bf16[256,3072]{1,0:T(8,128)(2,1)}, bf16[256,1024]{1,0:T(8,128)(2,1)}, bf16[256,5248]{1,0:T(8,128)(2,1)}, bf16[656,1024]{1,0:T(8,128)(2,1)}), (bf16[256,3072]{1,0:T(8,128)(2,1)}, bf16[256,1024]{1,0:T(8,128)(2,1)}, ...) | async-done | bytes 6127632 | tf_op jit(solution)/shard_map/psum | solution.py:331
  (617 shorter events, 283.4 us)
Async XLA Ops:
  7.2 51.5 %all-gather.9.cloned.1.call-start = ((), (), s32[]{:S(2)}) async-start(), calls=%async_computation.8 | async-start | bytes 7864320 | tf_op jit(solution)/shard_map/all_gather | solution.py:306
  7.9 203.4 %all-gather.19.cloned.1.call-start = ((), (), s32[]{:S(2)}) async-start(), calls=%async_computation.13 | async-start | bytes 2359296 | tf_op jit(solution)/shard_map/all_gather | solution.py:205
  14.6 49.0 %copy-start.76 = (f32[4,1,256]{2,1,0:T(1,128)}, f32[4,1,256]{2,1,0:T(1,128)S(1)}, u32[]{:S(2)}) copy-start(f32[4,1,256]{2,1,0:T(1,128)S(1)} %convert_element_type.286) | copy-start | bytes 12292
  15.8 46.7 %copy-start.98 = (f32[128]{0:T(128)}, f32[128]{0:T(128)S(1)}, u32[]{:S(2)}) copy-start(f32[128]{0:T(128)S(1)} %get-tuple-element.1246) | copy-start | bytes 1540
  15.8 47.8 %copy-start.102 = (f32[128]{0:T(128)}, f32[128]{0:T(128)S(1)}, u32[]{:S(2)}) copy-start(f32[128]{0:T(128)S(1)} %get-tuple-element.1245) | copy-start | bytes 1540
  16.6 47.1 %copy-start.108 = (f32[128]{0:T(128)}, f32[128]{0:T(128)S(1)}, u32[]{:S(2)}) copy-start(f32[128]{0:T(128)S(1)} %fusion.147) | copy-start | bytes 1540
  17.4 57.7 %copy-start.95 = (f32[128,32]{0,1:T(8,128)}, f32[128,32]{0,1:T(8,128)S(1)}, u32[]{:S(2)}) copy-start(f32[128,32]{0,1:T(8,128)S(1)} %get-tuple-element.1235) | copy-start | bytes 49156
  78.1 169.5 %all-gather.11.cloned.1.call-start = ((), (), s32[]{:S(2)}) async-start(), calls=%async_computation.9 | async-start | bytes 2359296 | tf_op jit(solution)/shard_map/all_gather | solution.py:205
  79.9 203.3 %all-gather.13.cloned.1.call-start = ((), (), s32[]{:S(2)}) async-start(), calls=%async_computation.10 | async-start | bytes 2621440 | tf_op jit(solution)/shard_map/all_gather | solution.py:307
  80.5 75.7 %copy-start.125 = (bf16[256]{0:T(256)(128)(2,1)S(1)}, bf16[256]{0:T(256)(128)(2,1)}, u32[]{:S(2)}) copy-start(bf16[256]{0:T(256)(128)(2,1)} %param.35) | copy-start | bytes 1540
  80.5 80.8 %copy-start.69 = (f32[1,128,16,32]{1,3,2,0:T(8,128)S(1)}, f32[1,128,16,32]{1,3,2,0:T(8,128)}, u32[]{:S(2)}) copy-start(f32[1,128,16,32]{1,3,2,0:T(8,128)} %get-tuple-element.1224) | copy-start | bytes 786436
  80.5 228.1 %all-gather.15.cloned.1.call-start = ((), (), s32[]{:S(2)}) async-start(), calls=%async_computation.11 | async-start | bytes 13434880 | tf_op jit(solution)/shard_map/all_gather | solution.py:308
  81.1 80.3 %copy-start.67 = (f32[1,128,16,32]{1,3,2,0:T(8,128)S(1)}, f32[1,128,16,32]{1,3,2,0:T(8,128)}, u32[]{:S(2)}) copy-start(f32[1,128,16,32]{1,3,2,0:T(8,128)} %get-tuple-element.1205) | copy-start | bytes 786436
  81.1 80.3 %copy-start.68 = (f32[1,128,16,32]{1,3,2,0:T(8,128)S(1)}, f32[1,128,16,32]{1,3,2,0:T(8,128)}, u32[]{:S(2)}) copy-start(f32[1,128,16,32]{1,3,2,0:T(8,128)} %get-tuple-element.1206) | copy-start | bytes 786436
  81.1 270.1 %all-gather.17.cloned.1.call-start = ((), (), s32[]{:S(2)}) async-start(), calls=%async_computation.12 | async-start | bytes 6717440 | tf_op jit(solution)/shard_map/all_gather | solution.py:309
  83.0 15.0 %collective-permute-start.7 = (bf16[1,128,1024]{2,1,0:T(8,128)(2,1)}, bf16[1,128,1024]{2,1,0:T(8,128)(2,1)S(1)}, u32[]{:S(2)}, u32[]{:S(2)}) collective-permute-start(bf16[1,128,1024]{2,1,0:T(8,128)(2,1)} %slice.226), channel_id=1, source_target_pairs={{0,4},{4,8},{8,12},{12,16},{16,20},{20,24},{24,28},{28,0},{1,5},{5... | collective-permute-start | bytes 786440 | tf_op jit(solution)/shard_map/ppermute | solution.py:19
  85.2 22.1 %collective-permute-start = (bf16[1,128,1024]{2,1,0:T(8,128)(2,1)}, bf16[1,128,1024]{2,1,0:T(8,128)(2,1)S(1)}, u32[]{:S(2)}, u32[]{:S(2)}) collective-permute-start(bf16[1,128,1024]{2,1,0:T(8,128)(2,1)} %slice.227), channel_id=1, source_target_pairs={{0,4},{4,8},{8,12},{12,16},{16,20},{20,24},{24,28},{28,0},{1,5},{5... | collective-permute-start | bytes 786440 | tf_op jit(solution)/shard_map/ppermute | solution.py:19
  97.9 18.7 %collective-permute-start.8 = (bf16[1,128,1024]{2,1,0:T(8,128)(2,1)S(1)}, bf16[1,128,1024]{2,1,0:T(8,128)(2,1)}, u32[]{:S(2)}, u32[]{:S(2)}) collective-permute-start(bf16[1,128,1024]{2,1,0:T(8,128)(2,1)S(1)} %collective-permute-done.7), channel_id=1, source_target_pairs={{0,4},{4,8},{8,12},{12,16},{16,20},{20,24},{24,28},{28,0},{1,5},{5... | collective-permute-start | bytes 786440 | tf_op jit(solution)/shard_map/ppermute | solution.py:19
  97.9 53.1 %collective-permute-start.11 = (bf16[1,128,1024]{2,1,0:T(8,128)(2,1)}, bf16[1,128,1024]{2,1,0:T(8,128)(2,1)}, u32[]{:S(2)}, u32[]{:S(2)}) collective-permute-start(bf16[1,128,1024]{2,1,0:T(8,128)(2,1)} %slice.226), channel_id=1, source_target_pairs={{0,28},{4,0},{8,4},{12,8},{16,12},{20,16},{24,20},{28,24},{1,29},{... | collective-permute-start | bytes 786440 | tf_op jit(solution)/shard_map/ppermute | solution.py:21
  102.6 48.5 %collective-permute-start.4 = (bf16[1,128,1024]{2,1,0:T(8,128)(2,1)}, bf16[1,128,1024]{2,1,0:T(8,128)(2,1)}, u32[]{:S(2)}, u32[]{:S(2)}) collective-permute-start(bf16[1,128,1024]{2,1,0:T(8,128)(2,1)} %slice.227), channel_id=1, source_target_pairs={{0,28},{4,0},{8,4},{12,8},{16,12},{20,16},{24,20},{28,24},{1,29},{... | collective-permute-start | bytes 786440 | tf_op jit(solution)/shard_map/ppermute | solution.py:21
  107.2 54.0 %copy-start.87 = (bf16[1,128,1024]{2,1,0:T(8,128)(2,1)}, bf16[1,128,1024]{2,1,0:T(8,128)(2,1)S(1)}, u32[]{:S(2)}) copy-start(bf16[1,128,1024]{2,1,0:T(8,128)(2,1)S(1)} %collective-permute-done) | copy-start | bytes 786436
  107.2 44.1 %collective-permute-start.1 = (bf16[1,128,1024]{2,1,0:T(8,128)(2,1)S(1)}, bf16[1,128,1024]{2,1,0:T(8,128)(2,1)}, u32[]{:S(2)}, u32[]{:S(2)}) collective-permute-start(bf16[1,128,1024]{2,1,0:T(8,128)(2,1)S(1)} %collective-permute-done), channel_id=1, source_target_pairs={{0,4},{4,8},{8,12},{12,16},{16,20},{20,24},{24,28},{28,0},{1,5},{5... | collective-permute-start | bytes 786440 | tf_op jit(solution)/shard_map/ppermute | solution.py:19
  116.6 36.6 %collective-permute-start.9 = (bf16[1,128,1024]{2,1,0:T(8,128)(2,1)}, bf16[1,128,1024]{2,1,0:T(8,128)(2,1)}, u32[]{:S(2)}, u32[]{:S(2)}) collective-permute-start(bf16[1,128,1024]{2,1,0:T(8,128)(2,1)} %collective-permute-done.8), channel_id=1, source_target_pairs={{0,4},{4,8},{8,12},{12,16},{16,20},{20,24},{24,28},{28,0},{1,5},{5... | collective-permute-start | bytes 786440 | tf_op jit(solution)/shard_map/ppermute | solution.py:19
  119.2 429.3 %reduce-scatter.31.cloned.1.call-start = ((), (), s32[]{:S(2)}) async-start(), calls=%async_computation.21 | async-start | bytes 2359296
  151.0 21.2 %collective-permute-start.12 = (bf16[1,128,1024]{2,1,0:T(8,128)(2,1)}, bf16[1,128,1024]{2,1,0:T(8,128)(2,1)}, u32[]{:S(2)}, u32[]{:S(2)}) collective-permute-start(bf16[1,128,1024]{2,1,0:T(8,128)(2,1)} %collective-permute-done.11), channel_id=1, source_target_pairs={{0,28},{4,0},{8,4},{12,8},{16,12},{20,16},{24,20},{28,24},{1,29},{... | collective-permute-start | bytes 786440 | tf_op jit(solution)/shard_map/ppermute | solution.py:21
  151.1 27.1 %collective-permute-start.5 = (bf16[1,128,1024]{2,1,0:T(8,128)(2,1)}, bf16[1,128,1024]{2,1,0:T(8,128)(2,1)}, u32[]{:S(2)}, u32[]{:S(2)}) collective-permute-start(bf16[1,128,1024]{2,1,0:T(8,128)(2,1)} %collective-permute-done.4), channel_id=1, source_target_pairs={{0,28},{4,0},{8,4},{12,8},{16,12},{20,16},{24,20},{28,24},{1,29},{... | collective-permute-start | bytes 786440 | tf_op jit(solution)/shard_map/ppermute | solution.py:21
  151.4 27.2 %collective-permute-start.2 = (bf16[1,128,1024]{2,1,0:T(8,128)(2,1)}, bf16[1,128,1024]{2,1,0:T(8,128)(2,1)}, u32[]{:S(2)}, u32[]{:S(2)}) collective-permute-start(bf16[1,128,1024]{2,1,0:T(8,128)(2,1)} %collective-permute-done.1), channel_id=1, source_target_pairs={{0,4},{4,8},{8,12},{12,16},{16,20},{20,24},{24,28},{28,0},{1,5},{5... | collective-permute-start | bytes 786440 | tf_op jit(solution)/shard_map/ppermute | solution.py:19
  153.2 29.6 %collective-permute-start.10 = (bf16[1,128,1024]{2,1,0:T(8,128)(2,1)}, bf16[1,128,1024]{2,1,0:T(8,128)(2,1)}, u32[]{:S(2)}, u32[]{:S(2)}) collective-permute-start(bf16[1,128,1024]{2,1,0:T(8,128)(2,1)} %collective-permute-done.9), channel_id=1, source_target_pairs={{0,4},{4,8},{8,12},{12,16},{16,20},{20,24},{24,28},{28,0},{1,5},{5... | collective-permute-start | bytes 786440 | tf_op jit(solution)/shard_map/ppermute | solution.py:19
  161.2 217.3 %copy-start.78 = (f32[4,1,256]{2,1,0:T(1,128)}, f32[4,1,256]{2,1,0:T(1,128)S(1)}, u32[]{:S(2)}) copy-start(f32[4,1,256]{2,1,0:T(1,128)S(1)} %convert_element_type.287) | copy-start | bytes 12292
  172.2 19.7 %collective-permute-start.13 = (bf16[1,128,1024]{2,1,0:T(8,128)(2,1)}, bf16[1,128,1024]{2,1,0:T(8,128)(2,1)S(1)}, u32[]{:S(2)}, u32[]{:S(2)}) collective-permute-start(bf16[1,128,1024]{2,1,0:T(8,128)(2,1)} %collective-permute-done.12), channel_id=1, source_target_pairs={{0,28},{4,0},{8,4},{12,8},{16,12},{20,16},{24,20},{28,24},{1,29},{... | collective-permute-start | bytes 786440 | tf_op jit(solution)/shard_map/ppermute | solution.py:21
  178.2 23.8 %collective-permute-start.6 = (bf16[1,128,1024]{2,1,0:T(8,128)(2,1)}, bf16[1,128,1024]{2,1,0:T(8,128)(2,1)}, u32[]{:S(2)}, u32[]{:S(2)}) collective-permute-start(bf16[1,128,1024]{2,1,0:T(8,128)(2,1)} %collective-permute-done.5), channel_id=1, source_target_pairs={{0,28},{4,0},{8,4},{12,8},{16,12},{20,16},{24,20},{28,24},{1,29},{... | collective-permute-start | bytes 786440 | tf_op jit(solution)/shard_map/ppermute | solution.py:21
  178.6 11.2 collective-permute-start.3
  285.6 93.0 %copy-start.110 = (f32[128]{0:T(128)}, f32[128]{0:T(128)S(1)}, u32[]{:S(2)}) copy-start(f32[128]{0:T(128)S(1)} %broadcast_multiply_fusion.2) | copy-start | bytes 1540
  286.4 92.1 %copy-start.20 = (f32[1,128,1024]{2,1,0:T(8,128)}, f32[1,128,1024]{2,1,0:T(8,128)S(1)}, u32[]{:S(2)}) copy-start(f32[1,128,1024]{2,1,0:T(8,128)S(1)} %get-tuple-element.1241) | copy-start | bytes 1572868
  286.4 92.1 %copy-start.100 = (f32[128]{0:T(128)}, f32[128]{0:T(128)S(1)}, u32[]{:S(2)}) copy-start(f32[128]{0:T(128)S(1)} %broadcast_multiply_fusion.4) | copy-start | bytes 1540
  286.7 91.9 %copy-start.114 = (f32[128]{0:T(128)}, f32[128]{0:T(128)S(1)}, u32[]{:S(2)}) copy-start(f32[128]{0:T(128)S(1)} %fusion.148) | copy-start | bytes 1540
  286.7 91.9 %copy-start.106 = (f32[128]{0:T(128)}, f32[128]{0:T(128)S(1)}, u32[]{:S(2)}) copy-start(f32[128]{0:T(128)S(1)} %fusion.146) | copy-start | bytes 1540
  444.4 138.3 %reduce-scatter.25.cloned.1.call-start = ((), (), s32[]{:S(2)}) async-start(), calls=%async_computation.18 | async-start | bytes 2359296
  509.7 144.1 %reduce-scatter.29.cloned.1.call-start = ((), (), s32[]{:S(2)}) async-start(), calls=%async_computation.20 | async-start | bytes 2359296
  523.1 200.9 %reduce-scatter.27.cloned.1.call-start = ((), (), s32[]{:S(2)}) async-start(), calls=%async_computation.19 | async-start | bytes 2359296
  536.6 223.1 %reduce-scatter.19.cloned.1.call-start = ((), (), s32[]{:S(2)}) async-start(), calls=%async_computation.15 | async-start | bytes 2621440 | tf_op jit(solution)/shard_map/reduce_scatter | solution.py:329
  540.4 272.0 %reduce-scatter.23.cloned.1.call-start = ((), (), s32[]{:S(2)}) async-start(), calls=%async_computation.17 | async-start | bytes 6717440 | tf_op jit(solution)/shard_map/reduce_scatter | solution.py:329
  547.2 326.1 %reduce-scatter.17.cloned.1.call-start = ((), (), s32[]{:S(2)}) async-start(), calls=%async_computation.14 | async-start | bytes 7864320 | tf_op jit(solution)/shard_map/reduce_scatter | solution.py:329
  550.2 179.8 %copy-start.61 = (bf16[1,128,1024]{1,2,0:T(8,128)(2,1)}, bf16[1,128,1024]{1,2,0:T(8,128)(2,1)S(1)}, u32[]{:S(2)}) copy-start(bf16[1,128,1024]{1,2,0:T(8,128)(2,1)S(1)} %copy.108) | copy-start | bytes 786436
  584.4 141.8 %copy-start.96 = (f32[128,32]{0,1:T(8,128)S(1)}, f32[128,32]{0,1:T(8,128)}, u32[]{:S(2)}) copy-start(f32[128,32]{0,1:T(8,128)} %copy-done.95) | copy-start | bytes 49156
  584.4 141.8 %copy-start.97 = (f32[128,32]{0,1:T(8,128)S(1)}, f32[128,32]{0,1:T(8,128)}, u32[]{:S(2)}) copy-start(f32[128,32]{0,1:T(8,128)} %get-tuple-element.1236) | copy-start | bytes 49156
  734.9 228.2 %reduce-scatter.21.cloned.1.call-start = ((), (), s32[]{:S(2)}) async-start(), calls=%async_computation.16 | async-start | bytes 13434880 | tf_op jit(solution)/shard_map/reduce_scatter | solution.py:329
  759.6 419.7 %all-reduce.19.cloned.1.call-start = ((), (), s32[]{:S(2)}) async-start(), calls=%async_computation.22 | async-start | bytes 12255232 | tf_op jit(solution)/shard_map/psum | solution.py:331
  (128 other events, 706.1 us)
Sparse Core Ops, SparseCore 0:
  9.6 49.0 all-gather.8
  78.3 75.0 all-gather.18
  155.4 57.6 all-gather.10
  214.6 20.7 all-gather.12
  236.8 71.6 all-gather.14
  309.9 41.1 all-gather.16
  444.4 67.8 reduce-scatter.30
  515.8 66.8 reduce-scatter.24
  586.8 66.8 reduce-scatter.28
  657.1 66.8 reduce-scatter.26
  726.5 30.4 reduce-scatter.18
  760.2 52.2 reduce-scatter.22
  814.9 58.3 reduce-scatter.16
  876.0 86.9 reduce-scatter.20
  968.3 211.0 all-reduce.18
